TPU v7x, 512 devices: a whole 4x8x8 slice. The times are simulated.
512 devices in a mesh: seq: 64 (over y, x, core), head: 8 (over z).
Axes of the slice: x: 4, y: 8, z: 8, core: 2. Of those that a mesh axis runs over, the one named last changes fastest.
Arguments:
- queries: bfloat16 [32768, 4096], P(('seq', 'head')), may hold values from -5 to 5
- new_keys: bfloat16 [32768, 1024], P(('seq', 'head')), may hold values from -12 to 12
- new_values: bfloat16 [32768, 1024], P(('seq', 'head')), may hold values from -6 to 6
- cache_keys: bfloat16 [131072, 1024], P('seq', 'head'), may hold values from -12 to 12
- cache_values: bfloat16 [131072, 1024], P('seq', 'head'), may hold values from -6 to 6
- tile_lists: int32 [256, 8, 12], P('seq', 'head'), may hold values from 0 to 1023, as said below
Outputs:
- attended: bfloat16 [32768, 4096], P(('seq', 'head'))
Inputs may be any that keep to these rules, and one draw needn't show every extreme that they name: `tile_lists`: for one key head, the 12 tiles of one block's list are distinct; the lists of the 4 blocks of one index of seq together name exactly 24 distinct tiles, at most 2 of them of one index of seq (tiles k * 16 to k * 16 + 15), and some index has exactly 2.
All inputs are finite; a program needn't handle non-finite values.
Results may differ from a plain program's by a relative error of at most 0.003.
Values may be sent and summed in bfloat16 or wider, within the bound.
A program may use at most 64 MiB of HBM per device.

v0:
```python
import math
import jax
import jax.numpy as jnp
from jax import lax
from jax.sharding import PartitionSpec as P

HQ = 32
KV = 8
HD = 128
QB = 128
TILE = 128
SEL = 12
NEG_FILL = -1e30


def passed_along(block, axis, distance):
    devices = range(lax.axis_size(axis))
    route = [(i - distance, i) for i in devices if i - distance in devices]
    return lax.ppermute(block, axis, route)


def pair_ranks(owners, tiles):
    pair_count = owners.shape[-1]
    earlier = jnp.arange(pair_count)[:, None] > jnp.arange(pair_count)[None, :]
    same_tile = tiles[..., :, None] == tiles[..., None, :]
    first_seen = jnp.logical_not(jnp.any(same_tile & earlier, axis=-1))
    same_owner = owners[..., :, None] == owners[..., None, :]
    smaller = tiles[..., None, :] < tiles[..., :, None]
    counted = same_owner & smaller & first_seen[..., None, :]
    return (jnp.sum(counted.astype(jnp.int32), axis=-1), first_seen)


def on_device(queries, new_keys, new_values, cache_keys, cache_values, tile_lists):
    q_rows, k_rows, v_rows = (
        lax.all_to_all(queries, "head", split_axis=1, concat_axis=0, tiled=True),
        lax.all_to_all(new_keys, "head", split_axis=1, concat_axis=0, tiled=True),
        lax.all_to_all(new_values, "head", split_axis=1, concat_axis=0, tiled=True),
    )
    rows_here = q_rows.shape[0]
    kv_here = k_rows.shape[1] // HD
    group_size = HQ // KV
    blocks_here = rows_here // QB
    tiles_here = cache_keys.shape[0] // TILE
    shards = lax.axis_size("seq")
    shard_index = lax.axis_index("seq")
    pair_total = blocks_here * SEL
    pool_size = max(SEL, pair_total // 2)
    capacity = max(2, (4 * pool_size + 3 * shards - 1) // (3 * shards))
    scale_factor = 1.0 / math.sqrt(HD)
    prior_keys, prior_values = passed_along(
        (k_rows[rows_here - QB :], v_rows[rows_here - QB :]), "seq", 1
    )
    pair_tiles = jnp.transpose(tile_lists, (1, 0, 2)).reshape(kv_here, pair_total)
    owners = pair_tiles // tiles_here
    pair_rank, first_seen = pair_ranks(owners, pair_tiles)
    every_list = lax.all_gather(tile_lists, "seq", axis=0, tiled=True)
    every_pair = jnp.transpose(
        every_list.reshape(shards, blocks_here, kv_here, SEL), (0, 2, 1, 3)
    ).reshape(shards, kv_here, pair_total)
    every_owner = every_pair // tiles_here
    every_rank, every_first = pair_ranks(every_owner, every_pair)
    own_hit = ((every_owner == shard_index) & every_first)[..., None]
    rank_hit = every_rank[..., None] == jnp.arange(capacity)
    marked = jnp.where(own_hit & rank_hit, (every_pair % tiles_here)[..., None] + 1, 0)
    asked_ids = jnp.sum(marked, axis=2) - 1
    head_pick = jnp.arange(kv_here)[None, :, None]
    filled = (asked_ids >= 0)[..., None, None]
    safe_ids = jnp.maximum(asked_ids, 0)
    key_tiles = jnp.transpose(cache_keys.reshape(tiles_here, TILE, kv_here, HD), (2, 0, 1, 3))
    value_tiles = jnp.transpose(cache_values.reshape(tiles_here, TILE, kv_here, HD), (2, 0, 1, 3))
    send_keys = jnp.where(filled, key_tiles[head_pick, safe_ids], jnp.zeros((), jnp.bfloat16))
    send_values = jnp.where(filled, value_tiles[head_pick, safe_ids], jnp.zeros((), jnp.bfloat16))
    causal = jnp.arange(QB)[:, None] >= jnp.arange(QB)[None, :]
    head_rows = jnp.arange(kv_here)[:, None]

    def local_part(block_index, source, prior_rows):
        current = lax.dynamic_slice_in_dim(source, block_index * QB, QB, 0)
        before_rows = lax.dynamic_slice_in_dim(source, jnp.maximum(block_index - 1, 0) * QB, QB, 0)
        previous = jnp.where(block_index == 0, prior_rows, before_rows)
        joined = jnp.concatenate([previous, current], axis=0).reshape(2 * QB, kv_here, HD)
        return jnp.transpose(joined, (1, 0, 2))

    def remote_part(block_index, received):
        block_owners = lax.dynamic_slice_in_dim(owners, block_index * SEL, SEL, 1)
        block_ranks = lax.dynamic_slice_in_dim(pair_rank, block_index * SEL, SEL, 1)
        return received[block_owners, head_rows, block_ranks].reshape(kv_here, SEL * TILE, HD)

    def block_weights(block_index, got_keys):
        query_block = lax.dynamic_slice_in_dim(q_rows, block_index * QB, QB, 0).reshape(
            QB, kv_here, group_size, HD
        )
        all_keys = jnp.concatenate(
            [remote_part(block_index, got_keys), local_part(block_index, k_rows, prior_keys)],
            axis=1,
        )
        scores = (
            jnp.einsum("qhgd,hkd->hgqk", query_block, all_keys, preferred_element_type=jnp.float32)
            * scale_factor
        )
        has_prior = jnp.broadcast_to((block_index > 0) | (shard_index > 0), (QB, QB))
        visible = jnp.concatenate(
            [jnp.ones((QB, SEL * TILE), dtype=bool), has_prior, causal], axis=1
        )
        masked = jnp.where(visible, scores, NEG_FILL)
        row_top = jnp.max(masked, axis=3, keepdims=True)
        exponent = jnp.exp(masked - row_top)
        row_total = jnp.sum(exponent, axis=3)
        return (exponent.astype(jnp.bfloat16), row_total)

    def block_output(block_index, weights, row_total, got_values):
        all_values = jnp.concatenate(
            [remote_part(block_index, got_values), local_part(block_index, v_rows, prior_values)],
            axis=1,
        )
        weighted = jnp.einsum(
            "hgqk,hkd->qhgd", weights, all_values, preferred_element_type=jnp.float32
        )
        result = weighted / jnp.transpose(row_total, (2, 0, 1))[..., None]
        return result.astype(jnp.bfloat16).reshape(QB, kv_here * group_size * HD)

    block_ids = jnp.arange(blocks_here)
    got_keys, got_values = (
        lax.all_to_all(send_keys, "seq", split_axis=0, concat_axis=0, tiled=True),
        lax.all_to_all(send_values, "seq", split_axis=0, concat_axis=0, tiled=True),
    )

    def whole_block(block_index):
        weights, row_total = block_weights(block_index, got_keys)
        return block_output(block_index, weights, row_total, got_values)

    outputs = lax.map(whole_block, block_ids)
    attended = outputs.reshape(rows_here, kv_here * group_size * HD)
    return lax.all_to_all(attended, "head", split_axis=0, concat_axis=1, tiled=True)


def solution(mesh):
    return jax.shard_map(
        on_device,
        mesh=mesh,
        in_specs=(
            P(("seq", "head"), None),
            P(("seq", "head"), None),
            P(("seq", "head"), None),
            P("seq", "head"),
            P("seq", "head"),
            P("seq", "head", None),
        ),
        out_specs=P(("seq", "head"), None),
        check_vma=False,
    )
```

profile of v0, /device:TPU:14, one launch (start us, length us, event | category | flops | bytes accessed | tf_op | source)
XLA Modules:
  0.0 396.6 jit_solution(17193188782176240120)
XLA Ops:
  0.0 1.6 copy_bitcast_fusion.2
  1.6 10.3 %all-to-all-start.1 = ((bf16[64,8,128]{2,0,1:T(8,128)(2,1)}), bf16[64,8,128]{2,0,1:T(8,128)(2,1)S(1)}, u32[]{:S(2)}, u32[]{:S(2)}) async-start(bf16[64,8,128]{2,0,1:T(8,128)(2,1)} %copy_bitcast_fusion.2), calls=%async_computation.1 | async-start | bytes 262144 | tf_op jit(solution)/shard_map/all_to_all | solution.py:37
  12.0 49.1 %all_gather.3 = s32[256,1,12]{2,1,0:T(1,128)S(1)} all-gather(s32[4,1,12]{2,1,0:T(1,128)} %param.13), channel_id=1, replica_groups=mesh['seq'=64,'head'=8] {'seq'}, dimensions={0}, use_global_device_ids=true | all-gather | bytes 12480 | tf_op jit(solution)/shard_map/all_gather | solution.py:56
  61.0 0.5 broadcast.762
  61.5 0.9 reduce.22
  62.6 0.5 and_reduce_fusion
  63.1 1.9 copy.90
  65.0 0.4 convert_reduce_fusion
  65.4 1.6 copy_bitcast_fusion.1
  67.0 7.2 %all-to-all-start.3 = ((bf16[64,8,128]{2,0,1:T(8,128)(2,1)}), bf16[64,8,128]{2,0,1:T(8,128)(2,1)S(1)}, u32[]{:S(2)}, u32[]{:S(2)}) async-start(bf16[64,8,128]{2,0,1:T(8,128)(2,1)} %copy_bitcast_fusion.1), calls=%async_computation.3 | async-start | bytes 262144 | tf_op jit(solution)/shard_map/all_to_all | solution.py:36
  74.2 9.6 %all-to-all-done.3 = bf16[64,8,128]{2,0,1:T(8,128)(2,1)S(1)} async-done(((bf16[64,8,128]{2,0,1:T(8,128)(2,1)}), bf16[64,8,128]{2,0,1:T(8,128)(2,1)S(1)}, u32[]{:S(2)}, u32[]{:S(2)}) %all-to-all-start.3) | async-done | bytes 131104 | tf_op jit(solution)/shard_map/all_to_all | solution.py:36
  83.8 3.5 all-to-all-start.4
  87.6 3.1 gather_fusion.2
  90.6 3.0 gather_fusion.3
  93.8 5.8 %broadcast_select_fusion = (bf16[64,1,2,128,128]{4,3,2,1,0:T(8,128)(2,1)}, bf16[64,1,2,128,128]{4,3,2,1,0:T(8,128)(2,1)}) fusion(bf16[64,1,2,128,128]{4,3,2,1,0:T(8,128)(2,1)} %bitcast.146, pred[64,2]{1,0:T(8,128)(4,1)S(1)} %copy.70, bf16[64,1,2,128,128]{4,3,2,1,0:T(8,128)(2,1)} %bitcast.145), kind=kLoop, calls=%fused_computation.42 | loop fusion | flops 4194304 | bytes 16777344 | tf_op jit(solution)/shard_map/jit(_where)/select_n | solution.py:71
  99.6 4.4 %all-to-all-done.4 = bf16[64,8,512]{2,0,1:T(8,128)(2,1)S(1)} async-done(((bf16[64,8,512]{2,0,1:T(8,128)(2,1)}), bf16[64,8,512]{2,0,1:T(8,128)(2,1)S(1)}, u32[]{:S(2)}, u32[]{:S(2)}) %all-to-all-start.4) | async-done | bytes 524320 | tf_op jit(solution)/shard_map/all_to_all | solution.py:35
  104.0 104.5 %all_to_all.86 = bf16[64,1,2,128,128]{4,3,2,1,0:T(8,128)(2,1)} all-to-all(bf16[64,1,2,128,128]{4,3,2,1,0:T(8,128)(2,1)} %get-tuple-element.300), channel_id=1, replica_groups=mesh['seq'=64,'head'=8] {'seq'}, dimensions={0} | all-to-all | bytes 8388608 | tf_op jit(solution)/shard_map/all_to_all | solution.py:124
  208.5 6.6 %all-to-all-start.2 = ((bf16[64,1,2,128,128]{4,3,2,1,0:T(8,128)(2,1)}), bf16[64,1,2,128,128]{4,3,2,1,0:T(8,128)(2,1)}, u32[]{:S(2)}, u32[]{:S(2)}) async-start(bf16[64,1,2,128,128]{4,3,2,1,0:T(8,128)(2,1)} %get-tuple-element.299), calls=%async_computation.2 | async-start | bytes 8388608 | tf_op jit(solution)/shard_map/all_to_all | solution.py:123
  215.1 0.6 reduce.21
  215.8 0.2 fusion.28
  216.1 2.1 collective-permute-start
  218.2 3.4 collective-permute-start.1
  221.5 0.2 convert_reduce_fusion.1
  221.7 4.7 %collective-permute-done = bf16[128,128]{1,0:T(8,128)(2,1)S(1)} collective-permute-done((bf16[128,128]{1,0:T(8,128)(2,1)S(1)}, bf16[128,128]{1,0:T(8,128)(2,1)S(1)}, u32[]{:S(2)}, u32[]{:S(2)}) %collective-permute-start) | collective-permute-done | bytes 32800 | tf_op jit(solution)/shard_map/ppermute | solution.py:19
  226.4 0.6 collective-permute-done.1
  227.0 83.4 %all-to-all-done.2 = bf16[64,1,2,128,128]{4,3,2,1,0:T(8,128)(2,1)} async-done(((bf16[64,1,2,128,128]{4,3,2,1,0:T(8,128)(2,1)}), bf16[64,1,2,128,128]{4,3,2,1,0:T(8,128)(2,1)}, u32[]{:S(2)}, u32[]{:S(2)}) %all-to-all-start.2) | async-done | bytes 4194336 | tf_op jit(solution)/shard_map/all_to_all | solution.py:123
  310.4 65.0 %while.13 = (s32[]{:T(128)}, bf16[4,128,512]{2,1,0:T(8,128)(2,1)S(1)}, s32[4]{0:T(128)S(1)}, s32[1,48]{1,0:T(1,128)S(1)}, s32[1,48]{1,0:T(1,128)S(1)}, /*index=5...) while((s32[]{:T(128)}, ...), condition=%wide.region_8.9_spmd.clone, body=%wide.region_5.8_spmd.clone.sunk | while | flops 478692352 | bytes 31508588 | solution.py:131
  310.4 0.6 dynamic_slice.81
  313.6 2.9 gather_fusion
  317.2 0.3 pad_add_fusion.5
  317.5 0.6 fusion.47
  318.2 1.9 copy-done.1
  320.0 0.5 fusion.48
  320.7 2.9 gather_fusion.1
  323.5 0.2 copy.97
  323.7 2.8 fusion.49
  326.7 0.6 dynamic_slice.81
  329.8 2.9 gather_fusion
  333.5 0.3 pad_add_fusion.5
  333.8 0.6 fusion.47
  334.4 1.9 copy-done.1
  336.3 0.5 fusion.48
  336.9 2.9 gather_fusion.1
  339.8 0.2 copy.97
  340.0 2.8 fusion.49
  342.9 0.6 dynamic_slice.81
  346.1 2.9 gather_fusion
  349.7 0.3 pad_add_fusion.5
  350.0 0.6 fusion.47
  350.7 1.9 copy-done.1
  352.5 0.5 fusion.48
  353.2 2.9 gather_fusion.1
  356.2 2.8 fusion.49
  359.2 0.6 dynamic_slice.81
  362.3 2.9 gather_fusion
  366.0 0.3 pad_add_fusion.5
  366.3 0.6 fusion.47
  366.9 1.9 copy-done.1
  368.8 0.5 fusion.48
  369.4 2.9 gather_fusion.1
  372.3 0.2 copy.97
  372.5 2.8 fusion.49
  375.4 20.3 %all_to_all.87 = bf16[8,64,512]{2,1,0:T(8,128)(2,1)S(1)} all-to-all(bf16[8,64,512]{2,1,0:T(8,128)(2,1)S(1)} %bitcast.157), channel_id=1, replica_groups=mesh['seq'=64,'head'=8] {'head'}, dimensions={0} | all-to-all | bytes 1048576 | tf_op jit(solution)/shard_map/all_to_all | solution.py:133
  395.7 0.8 copy.86
  (98 shorter events, 3.8 us)
Async XLA Ops:
  0.0 87.5 %copy-start = (bf16[2048,128]{1,0:T(8,128)(2,1)S(1)}, bf16[2048,128]{1,0:T(8,128)(2,1)}, u32[]{:S(2)}) copy-start(bf16[2048,128]{1,0:T(8,128)(2,1)} %param.12) | copy-start | bytes 1572868
  1.6 65.4 %all-to-all-start.1 = ((bf16[64,8,128]{2,0,1:T(8,128)(2,1)}), bf16[64,8,128]{2,0,1:T(8,128)(2,1)S(1)}, u32[]{:S(2)}, u32[]{:S(2)}) async-start(bf16[64,8,128]{2,0,1:T(8,128)(2,1)} %copy_bitcast_fusion.2), calls=%async_computation.1 | async-start | bytes 262144 | tf_op jit(solution)/shard_map/all_to_all | solution.py:37
  67.0 16.8 %all-to-all-start.3 = ((bf16[64,8,128]{2,0,1:T(8,128)(2,1)}), bf16[64,8,128]{2,0,1:T(8,128)(2,1)S(1)}, u32[]{:S(2)}, u32[]{:S(2)}) async-start(bf16[64,8,128]{2,0,1:T(8,128)(2,1)} %copy_bitcast_fusion.1), calls=%async_computation.3 | async-start | bytes 262144 | tf_op jit(solution)/shard_map/all_to_all | solution.py:36
  83.8 20.2 %all-to-all-start.4 = ((bf16[64,8,512]{2,0,1:T(8,128)(2,1)}), bf16[64,8,512]{2,0,1:T(8,128)(2,1)S(1)}, u32[]{:S(2)}, u32[]{:S(2)}) async-start(bf16[64,8,512]{2,0,1:T(8,128)(2,1)} %bitcast.99), calls=%async_computation.4 | async-start | bytes 1048576 | tf_op jit(solution)/shard_map/all_to_all | solution.py:35
  87.6 3.1 copy-start.2
  208.5 6.6 %copy-start.3 = (s32[4,1,12]{2,1,0:T(1,128)S(1)}, s32[4,1,12]{2,1,0:T(1,128)}, u32[]{:S(2)}) copy-start(s32[4,1,12]{2,1,0:T(1,128)} %param.13) | copy-start | bytes 580
  208.5 102.0 %all-to-all-start.2 = ((bf16[64,1,2,128,128]{4,3,2,1,0:T(8,128)(2,1)}), bf16[64,1,2,128,128]{4,3,2,1,0:T(8,128)(2,1)}, u32[]{:S(2)}, u32[]{:S(2)}) async-start(bf16[64,1,2,128,128]{4,3,2,1,0:T(8,128)(2,1)} %get-tuple-element.299), calls=%async_computation.2 | async-start | bytes 8388608 | tf_op jit(solution)/shard_map/all_to_all | solution.py:123
  216.1 10.3 %collective-permute-start = (bf16[128,128]{1,0:T(8,128)(2,1)S(1)}, bf16[128,128]{1,0:T(8,128)(2,1)S(1)}, u32[]{:S(2)}, u32[]{:S(2)}) collective-permute-start(bf16[128,128]{1,0:T(8,128)(2,1)S(1)} %bitcast.159), channel_id=1, source_target_pairs={{0,8},{8,16},{16,24},{24,32},{32,40},{40,48},{48,56},{56,64},{64,7... | collective-permute-start | bytes 98312 | tf_op jit(solution)/shard_map/ppermute | solution.py:19
  218.2 8.9 %collective-permute-start.1 = (bf16[128,128]{1,0:T(8,128)(2,1)S(1)}, bf16[128,128]{1,0:T(8,128)(2,1)S(1)}, u32[]{:S(2)}, u32[]{:S(2)}) collective-permute-start(bf16[128,128]{1,0:T(8,128)(2,1)S(1)} %bitcast.160), channel_id=1, source_target_pairs={{0,8},{8,16},{16,24},{24,32},{32,40},{40,48},{48,56},{56,64},{64,7... | collective-permute-start | bytes 98312 | tf_op jit(solution)/shard_map/ppermute | solution.py:19
  318.2 1.9 copy-start.1
  334.4 1.9 copy-start.1
  350.7 1.9 copy-start.1
  366.9 1.9 copy-start.1
where the time goes:
time: 398 us; the launch traced here: 397 us
  blocking collectives  174 us (44%)
  waiting for transfers between devices  103 us (26%)
  local copies, waits for them, and re-layouts  48.2 us (12%)
  starting transfers between devices  33 us (8%)
  matrix products  13.7 us (3%)
  other arithmetic  12.8 us (3%)
  loops' own time  12.1 us (3%)
    all_to_all x1, blocking collectives, on_device(): lax.all_to_all(send_values, 'seq', split_axis=0, concat_axis=0, tiled=True)  104 us
    all_to_all x1, waiting for transfers between devices, on_device(): lax.all_to_all(send_keys, 'seq', split_axis=0, concat_axis=0, tiled=True)  83.4 us
    all_gather x1, blocking collectives, on_device(): every_list = lax.all_gather(tile_lists, 'seq', axis=0, tiled=True)  49.1 us
    gather x8, local copies, waits for them, and re-layouts, remote_part(): received[block_owners, head_rows, block_ranks]  22.8 us
    all_to_all x1, blocking collectives, on_device(): lax.all_to_all(attended, 'head', split_axis=0, concat_axis=1, tiled=True)  20.3 us
    another operation x1, loops' own time, on_device(): outputs = lax.map(whole_block, block_ids)  12.1 us
    dot_general x4, matrix products, block_output(): jnp.einsum('hgqk,hkd->qhgd', weights, all_values, preferred_element_type=...  11.2 us
    all_to_all x1, starting transfers between devices, on_device(): lax.all_to_all(new_values, 'head', split_axis=1, concat_axis=0, tiled=True)  10.3 us
  transfers between devices with their start and end apart: 6, of which 5 were waited for; matrix products, arithmetic and copies ran while one was open for 5% of the time, Pallas kernels for 0%

commit v1 on v0

--- a/solution.py
+++ b/solution.py
@@ -53,7 +53,9 @@
     pair_tiles = jnp.transpose(tile_lists, (1, 0, 2)).reshape(kv_here, pair_total)
     owners = pair_tiles // tiles_here
     pair_rank, first_seen = pair_ranks(owners, pair_tiles)
-    every_list = lax.all_gather(tile_lists, "seq", axis=0, tiled=True)
+    every_list = jnp.concatenate(
+        lax.all_to_all(jnp.stack([tile_lists] * lax.axis_size("seq")), "seq", 0, 0), axis=0
+    )
     every_pair = jnp.transpose(
         every_list.reshape(shards, blocks_here, kv_here, SEL), (0, 2, 1, 3)
     ).reshape(shards, kv_here, pair_total)

time: 398 us -> 366 us (0.920)
  blocking collectives: 174 us -> 125 us
  waiting for transfers between devices: 103 us -> 111 us
  starting transfers between devices: 33 us -> 39.7 us
    all_gather x1 -> x0, blocking collectives: 49.1 us -> none  [on_device(): every_list = lax.all_gather(tile_lists, 'seq', axis=0, tiled=True)]
    all_to_all x0 -> x1, starting transfers between devices: none -> 10.5 us  [on_device(): lax.all_to_all(jnp.stack([tile_lists] * lax.axis_size('seq')), 'seq', 0, 0)]
    all_to_all x1, waiting for transfers between devices: 0.01 us -> 6.5 us  [on_device(): lax.all_to_all(new_values, 'head', split_axis=1, concat_axis=0, tiled=True)]
  transfers between devices with their start and end apart: 6 -> 7, of which waited for: 5 -> 7; matrix products, arithmetic and copies ran while one was open for 5% -> 6% of each run, Pallas kernels for 0% -> 0%
where the time goes in v1:
time: 366 us; the launch traced here: 364 us
  blocking collectives  125 us (34%)
  waiting for transfers between devices  111 us (30%)
  local copies, waits for them, and re-layouts  49.7 us (14%)
  starting transfers between devices  39.7 us (11%)
  matrix products  13.7 us (4%)
  other arithmetic  12.8 us (3%)
  loops' own time  12.1 us (3%)
    all_to_all x1, blocking collectives, on_device(): lax.all_to_all(send_values, 'seq', split_axis=0, concat_axis=0, tiled=True)  104 us
    all_to_all x1, waiting for transfers between devices, on_device(): lax.all_to_all(send_keys, 'seq', split_axis=0, concat_axis=0, tiled=True)  83.4 us
    gather x8, local copies, waits for them, and re-layouts, remote_part(): received[block_owners, head_rows, block_ranks]  22.8 us
    all_to_all x1, blocking collectives, on_device(): lax.all_to_all(attended, 'head', split_axis=0, concat_axis=1, tiled=True)  21.7 us
    another operation x1, loops' own time, on_device(): outputs = lax.map(whole_block, block_ids)  12.1 us
    dot_general x4, matrix products, block_output(): jnp.einsum('hgqk,hkd->qhgd', weights, all_values, preferred_element_type=...  11.2 us
    all_to_all x1, starting transfers between devices, on_device(): lax.all_to_all(jnp.stack([tile_lists] * lax.axis_size('seq')), 'seq', 0, 0)  10.5 us
    all_to_all x1, starting transfers between devices, on_device(): lax.all_to_all(new_values, 'head', split_axis=1, concat_axis=0, tiled=True)  10.3 us
  transfers between devices with their start and end apart: 7, of which 7 were waited for; matrix products, arithmetic and copies ran while one was open for 6% of the time, Pallas kernels for 0%

profile of v1, /device:TPU:14, one launch (start us, length us, event | category | flops | bytes accessed | tf_op | source)
XLA Modules:
  0.0 364.2 jit_solution(3538130317850450844)
XLA Ops:
  0.0 1.5 stack.2
  1.5 10.5 %all-to-all-start = ((s32[64,4,1,12]{3,2,1,0:T(1,128)}), s32[64,4,1,12]{3,2,1,0:T(1,128)S(1)}, u32[]{:S(2)}, u32[]{:S(2)}) async-start(s32[64,4,1,12]{3,2,1,0:T(1,128)} %stack.2), calls=%async_computation | async-start | bytes 262144 | tf_op jit(solution)/shard_map/all_to_all | solution.py:57
  12.0 1.6 copy_bitcast_fusion.2
  13.5 1.6 copy_bitcast_fusion.1
  15.1 1.9 copy.115
  17.0 3.8 %all-to-all-done = s32[64,4,1,12]{3,2,1,0:T(1,128)S(1)} async-done(((s32[64,4,1,12]{3,2,1,0:T(1,128)}), s32[64,4,1,12]{3,2,1,0:T(1,128)S(1)}, u32[]{:S(2)}, u32[]{:S(2)}) %all-to-all-start) | async-done | bytes 12320 | tf_op jit(solution)/shard_map/all_to_all | solution.py:57
  20.9 10.3 %all-to-all-start.2 = ((bf16[64,8,128]{2,0,1:T(8,128)(2,1)}), bf16[64,8,128]{2,0,1:T(8,128)(2,1)S(1)}, u32[]{:S(2)}, u32[]{:S(2)}) async-start(bf16[64,8,128]{2,0,1:T(8,128)(2,1)} %copy_bitcast_fusion.2), calls=%async_computation.2 | async-start | bytes 262144 | tf_op jit(solution)/shard_map/all_to_all | solution.py:37
  31.2 0.5 broadcast.765
  31.7 0.9 reduce.22
  32.8 0.5 and_reduce_fusion
  33.4 0.4 convert_reduce_fusion
  33.8 6.5 %all-to-all-done.2 = bf16[64,8,128]{2,0,1:T(8,128)(2,1)S(1)} async-done(((bf16[64,8,128]{2,0,1:T(8,128)(2,1)}), bf16[64,8,128]{2,0,1:T(8,128)(2,1)S(1)}, u32[]{:S(2)}, u32[]{:S(2)}) %all-to-all-start.2) | async-done | bytes 131104 | tf_op jit(solution)/shard_map/all_to_all | solution.py:37
  40.3 3.4 all-to-all-start.4
  43.7 9.0 %all-to-all-done.4 = bf16[64,8,128]{2,0,1:T(8,128)(2,1)S(1)} async-done(((bf16[64,8,128]{2,0,1:T(8,128)(2,1)}), bf16[64,8,128]{2,0,1:T(8,128)(2,1)S(1)}, u32[]{:S(2)}, u32[]{:S(2)}) %all-to-all-start.4) | async-done | bytes 131104 | tf_op jit(solution)/shard_map/all_to_all | solution.py:36
  52.6 3.5 all-to-all-start.5
  56.4 3.0 gather_fusion.3
  59.4 3.1 gather_fusion.2
  62.6 5.8 %broadcast_select_fusion = (bf16[64,1,2,128,128]{4,3,2,1,0:T(8,128)(2,1)}, bf16[64,1,2,128,128]{4,3,2,1,0:T(8,128)(2,1)}) fusion(bf16[64,1,2,128,128]{4,3,2,1,0:T(8,128)(2,1)} %bitcast.146, pred[64,2]{1,0:T(8,128)(4,1)S(1)} %copy.94, bf16[64,1,2,128,128]{4,3,2,1,0:T(8,128)(2,1)} %bitcast.147), kind=kLoop, calls=%fused_computation.42 | loop fusion | flops 4194304 | bytes 16777344 | tf_op jit(solution)/shard_map/jit(_where)/select_n | solution.py:73
  68.4 2.6 all-to-all-done.5
  71.1 103.6 %all_to_all.91 = bf16[64,1,2,128,128]{4,3,2,1,0:T(8,128)(2,1)} all-to-all(bf16[64,1,2,128,128]{4,3,2,1,0:T(8,128)(2,1)} %get-tuple-element.300), channel_id=1, replica_groups=mesh['seq'=64,'head'=8] {'seq'}, dimensions={0} | all-to-all | bytes 8388608 | tf_op jit(solution)/shard_map/all_to_all | solution.py:126
  174.6 6.6 %all-to-all-start.3 = ((bf16[64,1,2,128,128]{4,3,2,1,0:T(8,128)(2,1)}), bf16[64,1,2,128,128]{4,3,2,1,0:T(8,128)(2,1)}, u32[]{:S(2)}, u32[]{:S(2)}) async-start(bf16[64,1,2,128,128]{4,3,2,1,0:T(8,128)(2,1)} %get-tuple-element.299), calls=%async_computation.3 | async-start | bytes 8388608 | tf_op jit(solution)/shard_map/all_to_all | solution.py:125
  181.4 0.6 reduce.21
  182.3 2.1 collective-permute-start
  184.3 3.4 collective-permute-start.1
  187.7 0.2 convert_reduce_fusion.1
  187.9 4.7 %collective-permute-done = bf16[128,128]{1,0:T(8,128)(2,1)S(1)} collective-permute-done((bf16[128,128]{1,0:T(8,128)(2,1)S(1)}, bf16[128,128]{1,0:T(8,128)(2,1)S(1)}, u32[]{:S(2)}, u32[]{:S(2)}) %collective-permute-start) | collective-permute-done | bytes 32800 | tf_op jit(solution)/shard_map/ppermute | solution.py:19
  192.6 0.6 collective-permute-done.1
  193.2 83.4 %all-to-all-done.3 = bf16[64,1,2,128,128]{4,3,2,1,0:T(8,128)(2,1)} async-done(((bf16[64,1,2,128,128]{4,3,2,1,0:T(8,128)(2,1)}), bf16[64,1,2,128,128]{4,3,2,1,0:T(8,128)(2,1)}, u32[]{:S(2)}, u32[]{:S(2)}) %all-to-all-start.3) | async-done | bytes 4194336 | tf_op jit(solution)/shard_map/all_to_all | solution.py:125
  276.6 65.0 %while.13 = (s32[]{:T(128)}, bf16[4,128,512]{2,1,0:T(8,128)(2,1)S(1)}, s32[4]{0:T(128)S(1)}, s32[1,48]{1,0:T(1,128)S(1)}, s32[1,48]{1,0:T(1,128)S(1)}, /*index=5...) while((s32[]{:T(128)}, ...), condition=%wide.region_8.9_spmd.clone, body=%wide.region_5.8_spmd.clone.sunk | while | flops 478692352 | bytes 31508588 | solution.py:133
  276.6 0.6 dynamic_slice.81
  279.7 2.9 gather_fusion
  283.4 0.3 pad_add_fusion.5
  283.7 0.6 fusion.47
  284.4 1.9 copy-done.1
  286.2 0.5 fusion.48
  286.8 2.9 gather_fusion.1
  289.7 0.2 copy.122
  289.9 2.8 fusion.49
  292.8 0.6 dynamic_slice.81
  296.0 2.9 gather_fusion
  299.6 0.3 pad_add_fusion.5
  300.0 0.6 fusion.47
  300.6 1.9 copy-done.1
  302.5 0.5 fusion.48
  303.1 2.9 gather_fusion.1
  306.1 2.8 fusion.49
  309.1 0.6 dynamic_slice.81
  312.2 2.9 gather_fusion
  315.9 0.3 pad_add_fusion.5
  316.2 0.6 fusion.47
  316.9 1.9 copy-done.1
  318.7 0.5 fusion.48
  319.3 2.9 gather_fusion.1
  322.4 2.8 fusion.49
  325.4 0.6 dynamic_slice.81
  328.5 2.9 gather_fusion
  332.2 0.3 pad_add_fusion.5
  332.5 0.6 fusion.47
  333.1 1.9 copy-done.1
  335.0 0.5 fusion.48
  335.6 2.9 gather_fusion.1
  338.6 2.8 fusion.49
  341.6 21.7 %all_to_all.92 = bf16[8,64,512]{2,1,0:T(8,128)(2,1)S(1)} all-to-all(bf16[8,64,512]{2,1,0:T(8,128)(2,1)S(1)} %bitcast.158), channel_id=1, replica_groups=mesh['seq'=64,'head'=8] {'head'}, dimensions={0} | all-to-all | bytes 1048576 | tf_op jit(solution)/shard_map/all_to_all | solution.py:135
  363.3 0.8 copy.111
  (100 shorter events, 4.3 us)
Async XLA Ops:
  0.0 56.4 %copy-start = (bf16[2048,128]{1,0:T(8,128)(2,1)S(1)}, bf16[2048,128]{1,0:T(8,128)(2,1)}, u32[]{:S(2)}) copy-start(bf16[2048,128]{1,0:T(8,128)(2,1)} %param.11) | copy-start | bytes 1572868
  1.5 19.4 %all-to-all-start = ((s32[64,4,1,12]{3,2,1,0:T(1,128)}), s32[64,4,1,12]{3,2,1,0:T(1,128)S(1)}, u32[]{:S(2)}, u32[]{:S(2)}) async-start(s32[64,4,1,12]{3,2,1,0:T(1,128)} %stack.2), calls=%async_computation | async-start | bytes 262144 | tf_op jit(solution)/shard_map/all_to_all | solution.py:57
  20.9 19.4 %all-to-all-start.2 = ((bf16[64,8,128]{2,0,1:T(8,128)(2,1)}), bf16[64,8,128]{2,0,1:T(8,128)(2,1)S(1)}, u32[]{:S(2)}, u32[]{:S(2)}) async-start(bf16[64,8,128]{2,0,1:T(8,128)(2,1)} %copy_bitcast_fusion.2), calls=%async_computation.2 | async-start | bytes 262144 | tf_op jit(solution)/shard_map/all_to_all | solution.py:37
  40.3 12.4 %all-to-all-start.4 = ((bf16[64,8,128]{2,0,1:T(8,128)(2,1)}), bf16[64,8,128]{2,0,1:T(8,128)(2,1)S(1)}, u32[]{:S(2)}, u32[]{:S(2)}) async-start(bf16[64,8,128]{2,0,1:T(8,128)(2,1)} %copy_bitcast_fusion.1), calls=%async_computation.4 | async-start | bytes 262144 | tf_op jit(solution)/shard_map/all_to_all | solution.py:36
  52.6 18.5 %all-to-all-start.5 = ((bf16[64,8,512]{2,0,1:T(8,128)(2,1)}), bf16[64,8,512]{2,0,1:T(8,128)(2,1)S(1)}, u32[]{:S(2)}, u32[]{:S(2)}) async-start(bf16[64,8,512]{2,0,1:T(8,128)(2,1)} %bitcast.100), calls=%async_computation.5 | async-start | bytes 1048576 | tf_op jit(solution)/shard_map/all_to_all | solution.py:35
  56.4 3.0 copy-start.2
  174.6 6.6 %copy-start.3 = (s32[4,1,12]{2,1,0:T(1,128)S(1)}, s32[4,1,12]{2,1,0:T(1,128)}, u32[]{:S(2)}) copy-start(s32[4,1,12]{2,1,0:T(1,128)} %param.13) | copy-start | bytes 580
  174.6 102.0 %all-to-all-start.3 = ((bf16[64,1,2,128,128]{4,3,2,1,0:T(8,128)(2,1)}), bf16[64,1,2,128,128]{4,3,2,1,0:T(8,128)(2,1)}, u32[]{:S(2)}, u32[]{:S(2)}) async-start(bf16[64,1,2,128,128]{4,3,2,1,0:T(8,128)(2,1)} %get-tuple-element.299), calls=%async_computation.3 | async-start | bytes 8388608 | tf_op jit(solution)/shard_map/all_to_all | solution.py:125
  182.3 10.3 %collective-permute-start = (bf16[128,128]{1,0:T(8,128)(2,1)S(1)}, bf16[128,128]{1,0:T(8,128)(2,1)S(1)}, u32[]{:S(2)}, u32[]{:S(2)}) collective-permute-start(bf16[128,128]{1,0:T(8,128)(2,1)S(1)} %bitcast.160), channel_id=1, source_target_pairs={{0,8},{8,16},{16,24},{24,32},{32,40},{40,48},{48,56},{56,64},{64,7... | collective-permute-start | bytes 98312 | tf_op jit(solution)/shard_map/ppermute | solution.py:19
  184.3 8.9 %collective-permute-start.1 = (bf16[128,128]{1,0:T(8,128)(2,1)S(1)}, bf16[128,128]{1,0:T(8,128)(2,1)S(1)}, u32[]{:S(2)}, u32[]{:S(2)}) collective-permute-start(bf16[128,128]{1,0:T(8,128)(2,1)S(1)} %bitcast.161), channel_id=1, source_target_pairs={{0,8},{8,16},{16,24},{24,32},{32,40},{40,48},{48,56},{56,64},{64,7... | collective-permute-start | bytes 98312 | tf_op jit(solution)/shard_map/ppermute | solution.py:19
  284.3 1.9 copy-start.1
  300.6 1.9 copy-start.1
  316.8 1.9 copy-start.1
  333.1 1.9 copy-start.1
